TPU v7x, 32 devices: a whole 2x2x4 slice. The times are simulated.
32 devices in a mesh: fsdp: 8 (over z, x), head: 2 (over core), tensor: 2 (over y).
Axes of the slice: x: 2, y: 2, z: 4, core: 2. Of those that a mesh axis runs over, the one named last changes fastest.
Arguments:
- block_in: bfloat16 [4096, 1024], P('fsdp'), may hold values from -6 to 6
- cotangent: bfloat16 [4096, 1024], P('fsdp'), may hold values from -6 to 6
- norm_gain: float32 [1024], replicated, may hold values from 0.5 to 1.5
- w_x: bfloat16 [1024, 32, 64], P('fsdp', 'head', 'tensor'), may hold values from -0.1875 to 0.1875
- w_z: bfloat16 [1024, 32, 64], P('fsdp', 'head', 'tensor'), may hold values from -0.1875 to 0.1875
- w_bc: bfloat16 [1024, 2, 128], P('fsdp'), may hold values from -0.1875 to 0.1875
- w_dt: bfloat16 [1024, 32], P('fsdp', 'head'), may hold values from -0.1875 to 0.1875
- conv_x: float32 [32, 64, 4], P('head', 'tensor'), may hold values from -3 to 3
- conv_bc: float32 [2, 128, 4], replicated, may hold values from -3 to 3
- dt_bias: float32 [32], P('head'), may hold values from -6 to -2
- a_log: float32 [32], P('head'), may hold values from -1.5 to 0.5
- skip: float32 [32], P('head'), may hold values from 0.5 to 1.5
- gate_gain: float32 [32, 64], P('head', 'tensor'), may hold values from 0.5 to 1.5
- w_out: bfloat16 [32, 64, 1024], P('head', 'tensor', 'fsdp'), may hold values from -0.125 to 0.125
Outputs:
- block_out: bfloat16 [4096, 1024], P('fsdp')
- grad_in: float32 [4096, 1024], P('fsdp')
- grad_norm_gain: float32 [1024], replicated
- grad_w_x: float32 [1024, 32, 64], P('fsdp', 'head', 'tensor')
- grad_w_z: float32 [1024, 32, 64], P('fsdp', 'head', 'tensor')
- grad_w_bc: float32 [1024, 2, 128], P('fsdp')
- grad_w_dt: float32 [1024, 32], P('fsdp', 'head')
- grad_conv_x: float32 [32, 64, 4], P('head', 'tensor')
- grad_conv_bc: float32 [2, 128, 4], replicated
- grad_dt_bias: float32 [32], P('head')
- grad_a_log: float32 [32], P('head')
- grad_skip: float32 [32], P('head')
- grad_gate_gain: float32 [32, 64], P('head', 'tensor')
- grad_w_out: float32 [32, 64, 1024], P('head', 'tensor', 'fsdp')
All inputs are finite; a program needn't handle non-finite values.
Results may differ from a plain program's by a relative error of at most 0.011.
Values may be sent and summed in bfloat16 or wider, within the bound.
A program may use at most 128 MiB of HBM per device.

v0:
```python
from functools import partial
import jax
import jax.numpy as jnp
from jax import lax
from jax.sharding import PartitionSpec as P

SPAN = 256
EPSILON = 1e-05
PRECISE = lax.Precision.HIGHEST


def causal_conv(signal, kernel):
    taps = kernel.shape[1]
    length = signal.shape[0]
    padded = jnp.pad(signal, ((taps - 1, 0), (0, 0)))
    total = jnp.zeros_like(signal)
    for offset in range(taps):
        total = total + padded[offset : offset + length] * kernel[:, offset]
    return total


def conv_silu(signal, kernel):
    return jax.nn.silu(causal_conv(signal, kernel))


def silu_slope(value):
    sigma = jax.nn.sigmoid(value)
    return sigma * (1.0 + value * (1.0 - sigma))


def scan_spans(values, step_size, rate, b_maps, c_maps, block):
    length, head_count, channels = values.shape
    blocks = length // block
    logs = (step_size * rate).reshape(blocks, block, head_count)
    cums = jnp.cumsum(logs, axis=1)
    x_blocks = values.reshape(blocks, block, head_count, channels)
    dt_blocks = step_size.reshape(blocks, block, head_count)
    b_blocks = b_maps.reshape(blocks, block, -1)
    c_blocks = c_maps.reshape(blocks, block, -1)
    scores = jnp.einsum("cln,csn->cls", c_blocks, b_blocks, precision=PRECISE)
    causal = (jnp.arange(block)[:, None] >= jnp.arange(block)[None, :])[None, :, :, None]
    gaps = cums[:, :, None, :] - cums[:, None, :, :]
    decays = jnp.where(causal, jnp.exp(jnp.where(causal, gaps, 0.0)), 0.0)
    mixing = scores[..., None] * decays * dt_blocks[:, None, :, :]
    intra_part = jnp.einsum("clsh,cshp->clhp", mixing, x_blocks, precision=PRECISE)
    to_end = jnp.exp(cums[:, -1:, :] - cums) * dt_blocks
    states = jnp.einsum("csh,csn,cshp->chpn", to_end, b_blocks, x_blocks, precision=PRECISE)
    whole_decay = jnp.exp(cums[:, -1, :])
    carried = []
    running = jnp.zeros_like(states[0])
    for position in range(blocks):
        carried.append(running)
        running = running * whole_decay[position][:, None, None] + states[position]
    entering = jnp.stack(carried)
    inter_part = jnp.einsum(
        "cln,clh,chpn->clhp", c_blocks, jnp.exp(cums), entering, precision=PRECISE
    )
    return (intra_part + inter_part).reshape(length, head_count, channels)


def mixer(values, dt_raw, dt_bias, a_log, skip, b_maps, c_maps, block):
    step_size = jax.nn.softplus(dt_raw + dt_bias)
    rate = -jnp.exp(a_log)
    return scan_spans(values, step_size, rate, b_maps, c_maps, block) + skip[:, None] * values


def on_device(
    block_in,
    cotangent,
    norm_gain,
    w_x,
    w_z,
    w_bc,
    w_dt,
    conv_x,
    conv_bc,
    dt_bias,
    a_log,
    skip,
    gate_gain,
    w_out,
):
    length, model_width = block_in.shape
    head_count, head_width, taps = conv_x.shape
    state_size = conv_bc.shape[1]
    inner_width = head_count * head_width
    group_count = lax.axis_size("head") * lax.axis_size("tensor")
    full_inner = inner_width * group_count
    weights = (w_x, w_z, w_bc, w_dt, w_out)
    gathered = (
        lax.all_gather(weights[0], "fsdp", axis=0, tiled=True),
        lax.all_gather(weights[1], "fsdp", axis=0, tiled=True),
        lax.all_gather(weights[2], "fsdp", axis=0, tiled=True),
        lax.all_gather(weights[3], "fsdp", axis=0, tiled=True),
        lax.all_gather(weights[4], "fsdp", axis=2, tiled=True),
    )
    weight_x = gathered[0].reshape(model_width, inner_width)
    weight_z = gathered[1].reshape(model_width, inner_width)
    weight_bc = gathered[2].reshape(model_width, 2 * state_size)
    weight_dt = gathered[3]
    weight_out = gathered[4].reshape(inner_width, model_width)
    kernel_x = conv_x.reshape(inner_width, taps)
    kernel_bc = conv_bc.reshape(2 * state_size, taps)
    gain_flat = gate_gain.reshape(inner_width)
    features = block_in.astype(jnp.float32)
    scale_in = lax.rsqrt(jnp.mean(features * features, axis=1, keepdims=True) + EPSILON)
    normed = (features * scale_in * norm_gain).astype(jnp.bfloat16)
    x_raw = jnp.dot(normed, weight_x, preferred_element_type=jnp.float32)
    z_raw = jnp.dot(normed, weight_z, preferred_element_type=jnp.float32)
    bc_raw = jnp.dot(normed, weight_bc, preferred_element_type=jnp.float32)
    dt_raw = jnp.dot(normed, weight_dt, preferred_element_type=jnp.float32)
    x_act = conv_silu(x_raw, kernel_x).astype(jnp.bfloat16)
    bc_act = conv_silu(bc_raw, kernel_bc).astype(jnp.bfloat16)
    values = x_act.astype(jnp.float32).reshape(length, head_count, head_width)
    b_maps = bc_act[:, :state_size].astype(jnp.float32)
    c_maps = bc_act[:, state_size:].astype(jnp.float32)
    mixed = mixer(values, dt_raw, dt_bias, a_log, skip, b_maps, c_maps, SPAN).reshape(
        length, inner_width
    )
    gated = mixed * jax.nn.silu(z_raw)
    square_sum = lax.psum(jnp.sum(gated * gated, axis=1), ("head", "tensor"))
    scale_out = lax.rsqrt(square_sum / full_inner + EPSILON)[:, None]
    normed_out = (gated * scale_out * gain_flat).astype(jnp.bfloat16)
    partial_out = jnp.dot(normed_out, weight_out, preferred_element_type=jnp.float32)
    summed = lax.psum(partial_out, ("head", "tensor"))
    block_out = (summed + features).astype(jnp.bfloat16)
    again = (
        lax.all_gather(weights[0], "fsdp", axis=0, tiled=True),
        lax.all_gather(weights[1], "fsdp", axis=0, tiled=True),
        lax.all_gather(weights[2], "fsdp", axis=0, tiled=True),
        lax.all_gather(weights[3], "fsdp", axis=0, tiled=True),
        lax.all_gather(weights[4], "fsdp", axis=2, tiled=True),
    )
    back_x = again[0].reshape(model_width, inner_width)
    back_z = again[1].reshape(model_width, inner_width)
    back_bc = again[2].reshape(model_width, 2 * state_size)
    back_dt = again[3]
    back_out = again[4].reshape(inner_width, model_width)
    upstream = cotangent.astype(jnp.float32)
    d_normed_out = jnp.dot(cotangent, back_out.T, preferred_element_type=jnp.float32)
    g_w_out = jnp.dot(normed_out.T, cotangent, preferred_element_type=jnp.float32)
    g_gate_gain = jnp.sum(d_normed_out * gated * scale_out, axis=0)
    d_hat = d_normed_out * gain_flat
    inner_sum = lax.psum(jnp.sum(d_hat * gated, axis=1), ("head", "tensor"))[:, None]
    d_gated = scale_out * d_hat - gated * scale_out**3 * inner_sum / full_inner
    d_mixed = d_gated * jax.nn.silu(z_raw)
    d_z = (d_gated * mixed * silu_slope(z_raw)).astype(jnp.bfloat16)
    _, pullback = jax.vjp(
        partial(mixer, block=SPAN), values, dt_raw, dt_bias, a_log, skip, b_maps, c_maps
    )
    d_xs, d_dt, g_dt_bias, g_a_log, g_skip, d_b, d_c = pullback(
        d_mixed.reshape(length, head_count, head_width)
    )
    d_dt, g_dt_bias, g_a_log, g_skip = lax.psum((d_dt, g_dt_bias, g_a_log, g_skip), "tensor")
    d_bc = lax.psum(jnp.concatenate([d_b, d_c], axis=1), ("head", "tensor"))
    _, pull_x = jax.vjp(conv_silu, x_raw, kernel_x)
    d_x_raw, g_conv_x = pull_x(d_xs.reshape(length, inner_width))
    _, pull_bc = jax.vjp(conv_silu, bc_raw, kernel_bc)
    d_bc_raw, g_conv_bc = pull_bc(d_bc)
    d_x_b = d_x_raw.astype(jnp.bfloat16)
    d_bc_b = d_bc_raw.astype(jnp.bfloat16)
    d_dt_b = d_dt.astype(jnp.bfloat16)
    g_w_x = jnp.dot(normed.T, d_x_b, preferred_element_type=jnp.float32)
    g_w_z = jnp.dot(normed.T, d_z, preferred_element_type=jnp.float32)
    g_w_bc = jnp.dot(normed.T, d_bc_b, preferred_element_type=jnp.float32)
    g_w_dt = jnp.dot(normed.T, d_dt_b, preferred_element_type=jnp.float32)
    local_part = (
        jnp.dot(d_x_b, back_x.T, preferred_element_type=jnp.float32)
        + jnp.dot(d_z, back_z.T, preferred_element_type=jnp.float32)
        + jnp.dot(d_dt_b, back_dt.T, preferred_element_type=jnp.float32)
        * (1.0 / lax.axis_size("tensor"))
    )
    d_normed = lax.psum(local_part, ("head", "tensor")) + jnp.dot(
        d_bc_b, back_bc.T, preferred_element_type=jnp.float32
    )
    g_norm_gain = jnp.sum(d_normed * features * scale_in, axis=0)
    d_in_hat = d_normed * norm_gain
    grad_in = (
        scale_in * d_in_hat
        - features * scale_in**3 * jnp.mean(d_in_hat * features, axis=1, keepdims=True)
        + upstream
    )
    big_grads = (
        lax.psum_scatter(
            g_w_x.reshape(model_width, head_count, head_width),
            "fsdp",
            scatter_dimension=0,
            tiled=True,
        ),
        lax.psum_scatter(
            g_w_z.reshape(model_width, head_count, head_width),
            "fsdp",
            scatter_dimension=0,
            tiled=True,
        ),
        lax.psum_scatter(g_w_bc, "fsdp", scatter_dimension=0, tiled=True),
        lax.psum_scatter(g_w_dt, "fsdp", scatter_dimension=0, tiled=True),
        lax.psum_scatter(
            g_w_out.reshape(head_count, head_width, model_width),
            "fsdp",
            scatter_dimension=2,
            tiled=True,
        ),
    )
    owned_bc = big_grads[2].reshape(-1, 2, state_size)
    small = lax.psum(
        (
            g_norm_gain,
            g_conv_x.reshape(head_count, head_width, taps),
            g_conv_bc.reshape(2, state_size, taps),
            g_dt_bias,
            g_a_log,
            g_skip,
            g_gate_gain.reshape(head_count, head_width),
        ),
        "fsdp",
    )
    return (
        block_out,
        grad_in,
        small[0],
        big_grads[0],
        big_grads[1],
        owned_bc,
        big_grads[3],
        small[1],
        small[2],
        small[3],
        small[4],
        small[5],
        small[6],
        big_grads[4],
    )


def solution(mesh):
    return jax.shard_map(
        on_device,
        mesh=mesh,
        in_specs=(
            P("fsdp", None),
            P("fsdp", None),
            P(),
            P("fsdp", "head", "tensor"),
            P("fsdp", "head", "tensor"),
            P("fsdp", None, None),
            P("fsdp", "head"),
            P("head", "tensor", None),
            P(),
            P("head"),
            P("head"),
            P("head"),
            P("head", "tensor"),
            P("head", "tensor", "fsdp"),
        ),
        out_specs=(
            P("fsdp", None),
            P("fsdp", None),
            P(),
            P("fsdp", "head", "tensor"),
            P("fsdp", "head", "tensor"),
            P("fsdp", None, None),
            P("fsdp", "head"),
            P("head", "tensor", None),
            P(),
            P("head"),
            P("head"),
            P("head"),
            P("head", "tensor"),
            P("head", "tensor", "fsdp"),
        ),
        check_vma=False,
    )
```

profile of v0, /device:TPU:0, one launch (start us, length us, event | category | flops | bytes accessed | tf_op | source)
XLA Modules:
  0.0 668.9 jit_solution(9409954152697508148)
XLA Ops:
  8.0 0.7 all-gather.6.cloned.1.call-update
  10.8 1.6 fusion.22
  13.0 28.3 %all_gather.22 = bf16[1024,16]{0,1:T(8,128)(2,1)S(1)} all-gather(bf16[128,16]{0,1:T(8,128)(2,1)} %param.20), channel_id=1, replica_groups=mesh['fsdp'=8,'head'=2,'tensor'=2] {'fsdp'}, dimensions={0}, use_global_device_ids=true | all-gather | bytes 36864 | tf_op jit(solution)/shard_map/all_gather | solution.py:94
  41.3 2.3 broadcast_multiply_fusion.8
  43.6 1.2 reduce-window.14
  45.9 0.7 fusion.91
  48.1 32.0 %all_gather.21 = bf16[1024,2,128]{2,1,0:T(2,128)(2,1)S(1)} all-gather(bf16[128,2,128]{2,1,0:T(2,128)(2,1)S(1)} %copy-done.27), channel_id=1, replica_groups=mesh['fsdp'=8,'head'=2,'tensor'=2] {'fsdp'}, dimensions={0}, use_global_device_ids=true | all-gather | bytes 589824 | tf_op jit(solution)/shard_map/all_gather | solution.py:93
  80.1 0.8 copy-done.9
  81.4 1.1 multiply_convert_fusion.3
  82.9 2.2 fusion.105
  85.1 0.9 copy-done.4
  86.0 1.6 multiply_convert_fusion.2
  88.0 1.3 convolution_add_fusion.3
  90.0 6.3 fusion.38
  96.3 0.8 copy.135
  97.2 1.3 copy.136
  98.5 3.5 multiply_reduce_fusion.9
  102.1 7.9 %psum.112 = f32[512]{0:T(512)S(1)} all-reduce(f32[512]{0:T(512)S(1)} %get-tuple-element.106), channel_id=1, replica_groups=mesh['fsdp'=8,'head'=2,'tensor'=2] {'head','tensor'}, use_global_device_ids=true, to_apply=%region_4.5 | all-reduce | flops 512 | bytes 4096 | tf_op jit(solution)/shard_map/psum | solution.py:121
  110.0 25.5 %all-gather.8.cloned.1.call-done = bf16[16,32,1024]{2,1,0:T(8,128)(2,1)} async-done(((bf16[16,32,128]{2,1,0:T(8,128)(2,1)}), bf16[16,32,1024]{2,1,0:T(8,128)(2,1)}) %all-gather.8.cloned.1.call-update) | async-done | bytes 1048592 | tf_op jit(solution)/shard_map/all_gather | solution.py:95
  135.5 3.9 multiply_reduce_fusion.3
  139.4 7.5 %psum.114 = f32[512]{0:T(512)S(1)} all-reduce(f32[512]{0:T(512)S(1)} %get-tuple-element.77), channel_id=1, replica_groups=mesh['fsdp'=8,'head'=2,'tensor'=2] {'head','tensor'}, use_global_device_ids=true, to_apply=%region_7.8 | all-reduce | flops 512 | bytes 4096 | tf_op jit(solution)/shard_map/psum | solution.py:144
  146.9 4.2 fusion.45
  151.2 1.3 copy.137
  152.5 2.9 reshape_reshape.8
  155.4 1.9 multiply_reduce_fusion.1
  157.3 2.6 convolution_bitcast_fusion.1
  159.8 1.0 multiply_reduce_fusion.14
  160.8 2.6 convolution_bitcast_fusion.2
  164.0 11.4 %fusion.9 = (f32[2,256,16]{1,2,0:T(8,128)}, f32[2,256,16]{1,2,0:T(8,128)}, f32[2,256,16]{1,2,0:T(8,128)}, f32[2,256,256]{2,1,0:T(8,128)}) fusion(f32[2,256,16]{1,2,0:T(8,128)S(1)} %bitcast.241, f32[2,256,16]{1,2,0:T(8,128)S(1)} %copy-done.26, f32[2,256,256]{2,1,0:T(8,128)S(1)} %copy-done.20, pred[256,256]{1,0:T(8,128)(4,1)S(1)} %copy-done.29, ...), kind=kOutput, calls=%fused_computation.18 | convolution fusion | flops 836608000 | bytes 2850816 | tf_op jit(solution)/shard_map/transpose(jvp(clsh,cshp->clhp))/dot_general | solution.py:45
  175.5 8.0 %fusion.41 = f32[2,256,16,32]{1,3,2,0:T(8,128)} fusion(f32[2,256,16]{1,2,0:T(8,128)S(1)} %bitcast.242, f32[2,256,16]{1,2,0:T(8,128)S(1)} %copy-done.26, f32[2,256,256]{2,1,0:T(8,128)S(1)} %copy-done.20, pred[256,256]{1,0:T(8,128)(4,1)S(1)} %copy-done.29, f32[2,256,16,32]{1,3,2,0:T(8,128)S(1)} %fusion.58, f32[2,16,32,256]{3,0,2,1:T(2,128)S(1)} %bitcast.207, ...), kind=kOutput, calls=%fused_computation.48 | convolution fusion | flops 816316416 | bytes 3833856 | tf_op jit(solution)/shard_map/transpose(jvp(clsh,cshp->clhp))/dot_general | solution.py:45
  183.5 0.9 multiply_reduce_fusion.2
  184.7 2.1 fusion.93
  186.8 0.8 reduce_sum.252
  188.2 1.2 multiply_bitcast_fusion
  189.4 0.8 copy.145
  190.2 2.5 convolution_add_fusion.2
  192.7 2.2 convolution_add_fusion.1
  194.9 0.8 copy.140
  195.8 1.0 copy.178
  196.9 2.6 copy.141
  199.9 5.0 reduce-window.16
  205.3 3.6 fusion.118
  209.0 0.9 multiply_reduce_fusion.7
  211.7 2.0 fusion.117
  213.8 0.8 pad_maximum_fusion
  214.6 8.2 %all-reduce.25 = (bf16[512,16]{0,1:T(8,128)(2,1)S(1)}, f32[16]{0:T(128)S(1)}, f32[16]{0:T(128)S(1)}, f32[16]{0:T(128)S(1)}) all-reduce(f32[512,16]{0,1:T(8,128)S(1)} %get-tuple-element.105, f32[16]{0:T(128)S(1)} %get-tuple-element.104, f32[16]{0:T(128)S(1)} %negate_multiply_fusion, ...), channel_id=1, replica_groups=mesh['fsdp'=8,'head'=2,'tensor'=2] {'tensor'}, use_global_device_ids=true, to_apply=%region_15.16 | all-reduce | flops 8240 | bytes 49536 | tf_op jit(solution)/shard_map/psum | solution.py:154
  222.8 4.0 multiply_add_fusion
  227.0 92.6 %all-reduce.28.cloned.1.call-done = (f32[512,1024]{1,0:T(8,128)}, f32[512,1024]{1,0:T(8,128)}, f32[512,256]{1,0:T(8,128)}) async-done(((f32[512,1024]{1,0:T(8,128)}, f32[512,1024]{1,0:T(8,128)}, f32[512,256]{1,0:T(8,128)}), (f32[512,1024]{1,0:T(8,128)}, f32[512,1024]{1,0:T(8,128)}, f32[512,256]{1,0:T(8,128)})) %all-reduce.28.cloned.1.call-update) | async-done | bytes 4718608 | tf_op jit(solution)/shard_map/psum | solution.py:125
  319.5 1.6 multiply_reduce_fusion.13
  321.9 1.6 fusion.95
  323.5 1.1 fusion.82
  324.7 3.4 fusion.92
  328.1 1.0 copy-done.3
  329.1 2.2 fusion.97
  331.4 2.2 fusion.99
  333.8 2.6 fusion.31
  336.5 38.1 %all-reduce.23 = (f32[1024]{0:T(1024)}, f32[16,32,4]{1,0,2:T(8,128)S(1)}, f32[2,128,4]{1,2,0:T(4,128)}, f32[16]{0:T(128)}, f32[16]{0:T(128)}, /*index=5*/f32[16]{0:T(128)}, f32[16,32]{1,0:T(8,128)}) all-reduce(f32[1024]{0:T(1024)S(1)} %get-tuple-element.74, ...), channel_id=1, replica_groups=mesh['fsdp'=8,'head'=2,'tensor'=2] {'fsdp'}, use_global_device_ids=true, to_apply=%region_21.22 | all-reduce | flops 4656 | bytes 37248 | tf_op jit(solution)/shard_map/psum | solution.py:206
  375.3 4.3 fusion.28
  379.6 8.5 %reduce-scatter.10.cloned.1.call-done = f32[128,256]{1,0:T(8,128)} async-done(((f32[1024,256]{1,0:T(8,128)}), f32[128,256]{1,0:T(8,128)}) %reduce-scatter.10.cloned.1.call-update) | async-done | bytes 131088 | tf_op jit(solution)/shard_map/reduce_scatter | solution.py:196
  388.1 1.6 reshape.276
  389.7 55.8 %reduce-scatter.12.cloned.1.call-done = f32[128,16]{0,1:T(8,128)} async-done(((f32[1024,16]{0,1:T(8,128)}), f32[128,16]{0,1:T(8,128)}) %reduce-scatter.12.cloned.1.call-update) | async-done | bytes 8208 | tf_op jit(solution)/shard_map/reduce_scatter | solution.py:197
  445.5 72.4 %reduce-scatter.14.cloned.1.call-done = f32[16,32,128]{2,1,0:T(8,128)} async-done(((f32[16,32,1024]{2,1,0:T(8,128)}), f32[16,32,128]{2,1,0:T(8,128)}) %reduce-scatter.14.cloned.1.call-update) | async-done | bytes 262160 | tf_op jit(solution)/shard_map/reduce_scatter | solution.py:198
  517.9 72.0 %reduce-scatter.8.cloned.1.call-done = f32[128,16,32]{0,2,1:T(8,128)} async-done(((f32[1024,16,32]{0,2,1:T(8,128)}), f32[128,16,32]{0,2,1:T(8,128)}) %reduce-scatter.8.cloned.1.call-update) | async-done | bytes 262160 | tf_op jit(solution)/shard_map/reduce_scatter | solution.py:190
  590.0 72.1 %reduce-scatter.6.cloned.1.call-done = f32[128,16,32]{0,2,1:T(8,128)} async-done(((f32[1024,16,32]{0,2,1:T(8,128)}), f32[128,16,32]{0,2,1:T(8,128)}) %reduce-scatter.6.cloned.1.call-update) | async-done | bytes 262160 | tf_op jit(solution)/shard_map/reduce_scatter | solution.py:184
  (221 shorter events, 13.8 us)
Async XLA Ops:
  7.2 39.4 %copy-start.69 = (f32[16,32]{1,0:T(8,128)S(1)}, f32[16,32]{1,0:T(8,128)}, u32[]{:S(2)}) copy-start(f32[16,32]{1,0:T(8,128)} %param.26) | copy-start | bytes 6148
  7.2 39.5 %copy-start.70 = (f32[2,128,4]{1,2,0:T(4,128)S(1)}, f32[2,128,4]{1,2,0:T(4,128)}, u32[]{:S(2)}) copy-start(f32[2,128,4]{1,2,0:T(4,128)} %param.22) | copy-start | bytes 12292
  7.2 39.5 %copy-start.75 = (f32[16]{0:T(128)S(1)}, f32[16]{0:T(128)}, u32[]{:S(2)}) copy-start(f32[16]{0:T(128)} %param.25) | copy-start | bytes 196
  7.2 40.2 %copy-start.45 = (f32[16,32,4]{1,2,0:T(4,128)S(1)}, f32[16,32,4]{1,2,0:T(4,128)}, u32[]{:S(2)}) copy-start(f32[16,32,4]{1,2,0:T(4,128)} %param.21) | copy-start | bytes 24580
  7.2 40.9 %copy-start.27 = (bf16[128,2,128]{2,1,0:T(2,128)(2,1)S(1)}, bf16[128,2,128]{2,1,0:T(2,128)(2,1)}, u32[]{:S(2)}) copy-start(bf16[128,2,128]{2,1,0:T(2,128)(2,1)} %param.19) | copy-start | bytes 196612
  7.2 75.6 %all-gather.4.cloned.1.call-start = ((), (), s32[]{:S(2)}) async-start(), calls=%async_computation.5 | async-start | bytes 1179648 | tf_op jit(solution)/shard_map/all_gather | solution.py:91
  8.0 90.6 %all-gather.6.cloned.1.call-start = ((), (), s32[]{:S(2)}) async-start(), calls=%async_computation.6 | async-start | bytes 1179648 | tf_op jit(solution)/shard_map/all_gather | solution.py:92
  8.7 126.8 %all-gather.8.cloned.1.call-start = ((), (), s32[]{:S(2)}) async-start(), calls=%async_computation.7 | async-start | bytes 1179648 | tf_op jit(solution)/shard_map/all_gather | solution.py:95
  9.4 310.1 %all-reduce.28.cloned.1.call-start = ((), (), s32[]{:S(2)}) async-start(), calls=%async_computation.13 | async-start | bytes 9437184 | tf_op jit(solution)/shard_map/psum | solution.py:125
  10.8 35.8 %copy-start.73 = (f32[16]{0:T(128)}, f32[16]{0:T(128)S(1)}, u32[]{:S(2)}) copy-start(f32[16]{0:T(128)S(1)} %exponential_negate_fusion) | copy-start | bytes 196
  10.8 70.1 %copy-start = (bf16[512,1024]{1,0:T(8,128)(2,1)S(1)}, bf16[512,1024]{1,0:T(8,128)(2,1)}, u32[]{:S(2)}) copy-start(bf16[512,1024]{1,0:T(8,128)(2,1)} %param.14) | copy-start | bytes 3145732
  10.8 70.1 %copy-start.30 = (f32[1024]{0:T(1024)S(1)}, f32[1024]{0:T(1024)}, u32[]{:S(2)}) copy-start(f32[1024]{0:T(1024)} %param.16) | copy-start | bytes 12292
  13.0 85.6 %copy-start.32 = (f32[512]{0:T(512)}, f32[512]{0:T(512)S(1)}, u32[]{:S(2)}) copy-start(f32[512]{0:T(512)S(1)} %get-tuple-element.141) | copy-start | bytes 6148
  41.3 2.3 copy-start.23
  45.0 37.6 %copy-start.34 = (f32[2,16,2]{1,2,0:T(2,128)}, f32[2,16,2]{1,2,0:T(2,128)S(1)}, u32[]{:S(2)}) copy-start(f32[2,16,2]{1,2,0:T(2,128)S(1)} %slice.130) | copy-start | bytes 772
  45.0 44.9 %copy-start.25 = (f32[2,256,16]{1,2,0:T(8,128)}, f32[2,256,16]{1,2,0:T(8,128)S(1)}, u32[]{:S(2)}) copy-start(f32[2,256,16]{1,2,0:T(8,128)S(1)} %bitcast_bitcast_fusion.1) | copy-start | bytes 98308
  45.2 143.0 %copy-start.36 = (f32[2,16]{1,0:T(2,128)}, f32[2,16]{1,0:T(2,128)S(1)}, u32[]{:S(2)}) copy-start(f32[2,16]{1,0:T(2,128)S(1)} %slice_reduce_fusion.2) | copy-start | bytes 388
  46.6 137.8 %copy-start.38 = (f32[512]{0:T(512)}, f32[512]{0:T(512)S(1)}, u32[]{:S(2)}) copy-start(f32[512]{0:T(512)S(1)} %mul.547) | copy-start | bytes 6148
  46.7 35.9 %copy-start.60 = (f32[256,1]{0,1:T(1,128)}, f32[256,1]{0,1:T(1,128)S(1)}, u32[]{:S(2)}) copy-start(f32[256,1]{0,1:T(1,128)S(1)} %get-tuple-element.136) | copy-start | bytes 3076
  46.7 35.9 %copy-start.62 = (f32[256,1]{0,1:T(1,128)}, f32[256,1]{0,1:T(1,128)S(1)}, u32[]{:S(2)}) copy-start(f32[256,1]{0,1:T(1,128)S(1)} %get-tuple-element.137) | copy-start | bytes 3076
  46.7 35.9 %copy-start.64 = (f32[256,1]{0,1:T(1,128)}, f32[256,1]{0,1:T(1,128)S(1)}, u32[]{:S(2)}) copy-start(f32[256,1]{0,1:T(1,128)S(1)} %get-tuple-element.138) | copy-start | bytes 3076
  46.7 35.8 %copy-start.66 = (f32[256,1]{0,1:T(1,128)}, f32[256,1]{0,1:T(1,128)S(1)}, u32[]{:S(2)}) copy-start(f32[256,1]{0,1:T(1,128)S(1)} %get-tuple-element.139) | copy-start | bytes 3076
  47.5 37.5 %copy-start.50 = (f32[512,1]{0,1:T(1,128)}, f32[512,1]{0,1:T(1,128)S(1)}, u32[]{:S(2)}) copy-start(f32[512,1]{0,1:T(1,128)S(1)} %get-tuple-element.132) | copy-start | bytes 6148
  47.6 37.5 %copy-start.52 = (f32[512,1]{0,1:T(1,128)}, f32[512,1]{0,1:T(1,128)S(1)}, u32[]{:S(2)}) copy-start(f32[512,1]{0,1:T(1,128)S(1)} %get-tuple-element.133) | copy-start | bytes 6148
  47.6 37.5 %copy-start.54 = (f32[512,1]{0,1:T(1,128)}, f32[512,1]{0,1:T(1,128)S(1)}, u32[]{:S(2)}) copy-start(f32[512,1]{0,1:T(1,128)S(1)} %get-tuple-element.134) | copy-start | bytes 6148
  47.6 37.5 %copy-start.56 = (f32[512,1]{0,1:T(1,128)}, f32[512,1]{0,1:T(1,128)S(1)}, u32[]{:S(2)}) copy-start(f32[512,1]{0,1:T(1,128)S(1)} %get-tuple-element.135) | copy-start | bytes 6148
  82.8 7.1 %copy-start.19 = (f32[2,256,256]{2,1,0:T(8,128)}, f32[2,256,256]{2,1,0:T(8,128)S(1)}, u32[]{:S(2)}) copy-start(f32[2,256,256]{2,1,0:T(8,128)S(1)} %fusion.116) | copy-start | bytes 1572868
  87.6 11.0 %copy-start.2 = (bf16[512,512]{1,0:T(8,128)(2,1)}, bf16[512,512]{1,0:T(8,128)(2,1)S(1)}, u32[]{:S(2)}) copy-start(bf16[512,512]{1,0:T(8,128)(2,1)S(1)} %get-tuple-element.108) | copy-start | bytes 1572868
  87.9 8.4 %copy-start.10 = (bf16[2,256,16,32]{1,0,3,2:T(2,128)(2,1)}, bf16[2,256,16,32]{1,0,3,2:T(2,128)(2,1)S(1)}, u32[]{:S(2)}) copy-start(bf16[2,256,16,32]{1,0,3,2:T(2,128)(2,1)S(1)} %reshape_reshape.7) | copy-start | bytes 1572868
  89.8 6.4 copy-start.8
  110.0 74.5 %copy-start.40 = (f32[512]{0:T(512)}, f32[512]{0:T(512)S(1)}, u32[]{:S(2)}) copy-start(f32[512]{0:T(512)S(1)} %get-tuple-element.143) | copy-start | bytes 6148
  157.2 3.6 copy-start.11
  157.2 3.6 copy-start.49
  159.8 4.2 copy-start.20
  159.8 4.2 copy-start.26
  159.8 4.2 copy-start.29
  159.8 4.2 copy-start.47
  190.2 4.7 copy-start.16
  195.8 3.7 copy-start.35
  195.8 3.7 copy-start.37
  195.8 4.0 copy-start.42
  195.8 3.9 copy-start.43
  195.8 3.9 copy-start.44
  195.8 9.3 %copy-start.48 = (f32[512,16]{0,1:T(8,128)S(1)}, f32[512,16]{0,1:T(8,128)}, u32[]{:S(2)}) copy-start(f32[512,16]{0,1:T(8,128)} %get-tuple-element.144) | copy-start | bytes 98308
  195.8 9.3 %copy-start.74 = (f32[16]{0:T(128)S(1)}, f32[16]{0:T(128)}, u32[]{:S(2)}) copy-start(f32[16]{0:T(128)} %copy-done.73) | copy-start | bytes 196
  195.8 9.5 %copy-start.76 = (f32[16]{0:T(128)S(1)}, f32[16]{0:T(128)}, u32[]{:S(2)}) copy-start(f32[16]{0:T(128)} %param.24) | copy-start | bytes 196
  199.8 9.1 %copy-start.59 = (f32[512]{0:T(512)S(1)}, f32[512]{0:T(512)}, u32[]{:S(2)}) copy-start(f32[512]{0:T(512)} %mul.539) | copy-start | bytes 6148
  205.0 4.0 copy-start.5
  205.0 4.0 copy-start.6
  205.0 4.0 copy-start.7
  211.7 2.9 copy-start.71
  211.7 11.1 %copy-start.24 = (bf16[1024,16]{0,1:T(8,128)(2,1)S(1)}, bf16[1024,16]{0,1:T(8,128)(2,1)}, u32[]{:S(2)}) copy-start(bf16[1024,16]{0,1:T(8,128)(2,1)} %copy-done.23) | copy-start | bytes 98308
  226.8 92.7 %copy-start.13 = (f32[512,256]{1,0:T(8,128)S(1)}, f32[512,256]{1,0:T(8,128)}, u32[]{:S(2)}) copy-start(f32[512,256]{1,0:T(8,128)} %copy-done.12) | copy-start | bytes 1572868
  226.9 94.3 %copy-start.61 = (f32[256,1]{0,1:T(1,128)S(1)}, f32[256,1]{0,1:T(1,128)}, u32[]{:S(2)}) copy-start(f32[256,1]{0,1:T(1,128)} %copy-done.60) | copy-start | bytes 3076
  226.9 94.3 %copy-start.63 = (f32[256,1]{0,1:T(1,128)S(1)}, f32[256,1]{0,1:T(1,128)}, u32[]{:S(2)}) copy-start(f32[256,1]{0,1:T(1,128)} %copy-done.62) | copy-start | bytes 3076
  226.9 94.3 %copy-start.65 = (f32[256,1]{0,1:T(1,128)S(1)}, f32[256,1]{0,1:T(1,128)}, u32[]{:S(2)}) copy-start(f32[256,1]{0,1:T(1,128)} %copy-done.64) | copy-start | bytes 3076
  226.9 94.3 %copy-start.67 = (f32[256,1]{0,1:T(1,128)S(1)}, f32[256,1]{0,1:T(1,128)}, u32[]{:S(2)}) copy-start(f32[256,1]{0,1:T(1,128)} %copy-done.66) | copy-start | bytes 3076
  226.9 161.2 %reduce-scatter.10.cloned.1.call-start = ((), (), s32[]{:S(2)}) async-start(), calls=%async_computation.10 | async-start | bytes 1179648 | tf_op jit(solution)/shard_map/reduce_scatter | solution.py:196
  323.5 122.0 %reduce-scatter.12.cloned.1.call-start = ((), (), s32[]{:S(2)}) async-start(), calls=%async_computation.11 | async-start | bytes 73728 | tf_op jit(solution)/shard_map/reduce_scatter | solution.py:197
  324.6 193.3 %reduce-scatter.14.cloned.1.call-start = ((), (), s32[]{:S(2)}) async-start(), calls=%async_computation.12 | async-start | bytes 2359296 | tf_op jit(solution)/shard_map/reduce_scatter | solution.py:198
  328.1 261.9 %reduce-scatter.8.cloned.1.call-start = ((), (), s32[]{:S(2)}) async-start(), calls=%async_computation.9 | async-start | bytes 2359296 | tf_op jit(solution)/shard_map/reduce_scatter | solution.py:190
  331.4 2.3 copy-start.72
  331.4 330.7 %reduce-scatter.6.cloned.1.call-start = ((), (), s32[]{:S(2)}) async-start(), calls=%async_computation.8 | async-start | bytes 2359296 | tf_op jit(solution)/shard_map/reduce_scatter | solution.py:184
  333.8 41.4 %copy-start.68 = (f32[512]{0:T(512)S(1)}, f32[512]{0:T(512)}, u32[]{:S(2)}) copy-start(f32[512]{0:T(512)} %get-tuple-element.140) | copy-start | bytes 6148
  (22 other events, 28.1 us)
Sparse Core Ops, SparseCore 0:
  10.1 43.5 all-gather.3
  55.8 39.1 all-gather.5
  97.1 38.3 all-gather.7
  227.0 92.4 all-reduce.27
  323.6 64.4 reduce-scatter.9
  391.7 53.8 reduce-scatter.11
  449.6 68.2 reduce-scatter.13
  522.0 67.8 reduce-scatter.7
  594.1 67.9 reduce-scatter.5
where the time goes:
time: 679 us; the launch traced here: 669 us
  waiting for transfers between devices  401 us (59%)
  blocking collectives  122 us (18%)
  matrix products  76.5 us (11%)
  other arithmetic  32.2 us (5%)
  local copies, waits for them, and re-layouts  21.5 us (3%)
  between operations  15 us (2%)
    psum x1, waiting for transfers between devices, on_device(): summed = lax.psum(partial_out, ('head', 'tensor'))  92.6 us
    reduce_scatter x1, waiting for transfers between devices, on_device(): lax.psum_scatter(g_w_out.reshape(head_count, head_width, model_width), 'f...  72.4 us
    reduce_scatter x1, waiting for transfers between devices, on_device(): lax.psum_scatter(g_w_x.reshape(model_width, head_count, head_width), 'fsd...  72.1 us
    reduce_scatter x1, waiting for transfers between devices, on_device(): lax.psum_scatter(g_w_z.reshape(model_width, head_count, head_width), 'fsd...  72 us
    reduce_scatter x1, waiting for transfers between devices, on_device(): lax.psum_scatter(g_w_dt, 'fsdp', scatter_dimension=0, tiled=True)  55.8 us
    psum x1, blocking collectives, on_device(): lax.psum((g_norm_gain, g_conv_x.reshape(head_count, head_width, taps), g_...  38.1 us
    all_gather x1, blocking collectives, on_device(): lax.all_gather(weights[2], 'fsdp', axis=0, tiled=True)  32 us
    all_gather x1, blocking collectives, on_device(): lax.all_gather(weights[3], 'fsdp', axis=0, tiled=True)  28.3 us
  transfers between devices with their start and end apart: 9, of which 7 were waited for; matrix products, arithmetic and copies ran while one was open for 7% of the time, Pallas kernels for 0%

commit v1 on v0

--- a/solution.py
+++ b/solution.py
@@ -122,7 +122,7 @@
     scale_out = lax.rsqrt(square_sum / full_inner + EPSILON)[:, None]
     normed_out = (gated * scale_out * gain_flat).astype(jnp.bfloat16)
     partial_out = jnp.dot(normed_out, weight_out, preferred_element_type=jnp.float32)
-    summed = lax.psum(partial_out, ("head", "tensor"))
+    summed = jnp.sum(lax.all_gather(partial_out, ("head", "tensor")), axis=0)
     block_out = (summed + features).astype(jnp.bfloat16)
     again = (
         lax.all_gather(weights[0], "fsdp", axis=0, tiled=True),

time: 679 us -> 703 us (1.035)
  waiting for transfers between devices: 401 us -> 417 us
  other arithmetic: 32.2 us -> 41.9 us
    all_gather x0 -> x1, waiting for transfers between devices: none -> 57.6 us  [on_device(): summed = jnp.sum(lax.all_gather(partial_out, ('head', 'tensor')), axis=0)]
    psum x1, waiting for transfers between devices: 92.6 us -> 58.5 us  [on_device(): lax.psum(local_part, ('head', 'tensor'))]
    reduce_scatter x1, waiting for transfers between devices: 55.8 us -> 48.3 us  [on_device(): lax.psum_scatter(g_w_dt, 'fsdp', scatter_dimension=0, tiled=True)]
  transfers between devices with their start and end apart: 9 -> 10, of which waited for: 7 -> 8; matrix products, arithmetic and copies ran while one was open for 7% -> 8% of each run, Pallas kernels for 0% -> 0%
where the time goes in v1:
time: 703 us; the launch traced here: 693 us
  waiting for transfers between devices  417 us (59%)
  blocking collectives  122 us (17%)
  matrix products  75.1 us (11%)
  other arithmetic  41.9 us (6%)
  local copies, waits for them, and re-layouts  21 us (3%)
  between operations  15.4 us (2%)
    reduce_scatter x1, waiting for transfers between devices, on_device(): lax.psum_scatter(g_w_z.reshape(model_width, head_count, head_width), 'fsd...  72.1 us
    reduce_scatter x1, waiting for transfers between devices, on_device(): lax.psum_scatter(g_w_x.reshape(model_width, head_count, head_width), 'fsd...  72.1 us
    reduce_scatter x1, waiting for transfers between devices, on_device(): lax.psum_scatter(g_w_out.reshape(head_count, head_width, model_width), 'f...  72 us
    psum x1, waiting for transfers between devices, on_device(): lax.psum(local_part, ('head', 'tensor'))  58.5 us
    all_gather x1, waiting for transfers between devices, on_device(): summed = jnp.sum(lax.all_gather(partial_out, ('head', 'tensor')), axis=0)  57.6 us
    reduce_scatter x1, waiting for transfers between devices, on_device(): lax.psum_scatter(g_w_dt, 'fsdp', scatter_dimension=0, tiled=True)  48.3 us
    psum x1, blocking collectives, on_device(): lax.psum((g_norm_gain, g_conv_x.reshape(head_count, head_width, taps), g_...  38.3 us
    all_gather x1, blocking collectives, on_device(): lax.all_gather(weights[2], 'fsdp', axis=0, tiled=True)  31.7 us
  transfers between devices with their start and end apart: 10, of which 8 were waited for; matrix products, arithmetic and copies ran while one was open for 8% of the time, Pallas kernels for 0%

profile of v1, /device:TPU:0, one launch (start us, length us, event | category | flops | bytes accessed | tf_op | source)
XLA Modules:
  0.0 692.9 jit_solution(16199950182695180054)
XLA Ops:
  8.0 0.7 all-gather.8.cloned.1.call-update
  9.5 1.6 fusion.22
  11.6 28.1 %all_gather.28 = bf16[1024,16]{0,1:T(8,128)(2,1)S(1)} all-gather(bf16[128,16]{0,1:T(8,128)(2,1)} %param.20), channel_id=1, replica_groups=mesh['fsdp'=8,'head'=2,'tensor'=2] {'fsdp'}, dimensions={0}, use_global_device_ids=true | all-gather | bytes 36864 | tf_op jit(solution)/shard_map/all_gather | solution.py:94
  40.4 2.3 broadcast_multiply_fusion.8
  42.8 1.2 reduce-window.14
  44.4 0.7 fusion.91
  47.0 31.7 %all_gather.27 = bf16[1024,2,128]{2,1,0:T(2,128)(2,1)S(1)} all-gather(bf16[128,2,128]{2,1,0:T(2,128)(2,1)S(1)} %copy-done.22), channel_id=1, replica_groups=mesh['fsdp'=8,'head'=2,'tensor'=2] {'fsdp'}, dimensions={0}, use_global_device_ids=true | all-gather | bytes 589824 | tf_op jit(solution)/shard_map/all_gather | solution.py:93
  78.7 0.8 copy-done.7
  80.1 1.1 multiply_convert_fusion.3
  82.9 2.2 fusion.105
  85.1 0.9 copy-done.4
  86.0 1.6 multiply_convert_fusion.2
  88.0 1.3 convolution_add_fusion.3
  90.0 6.3 fusion.38
  96.4 0.8 copy.135
  97.3 1.3 copy.136
  98.6 3.6 multiply_reduce_fusion.9
  102.2 8.1 %psum.105 = f32[512]{0:T(512)S(1)} all-reduce(f32[512]{0:T(512)S(1)} %get-tuple-element.105), channel_id=1, replica_groups=mesh['fsdp'=8,'head'=2,'tensor'=2] {'head','tensor'}, use_global_device_ids=true, to_apply=%region_4.5 | all-reduce | flops 512 | bytes 4096 | tf_op jit(solution)/shard_map/psum | solution.py:121
  110.2 24.5 %all-gather.10.cloned.1.call-done = bf16[16,32,1024]{2,1,0:T(8,128)(2,1)} async-done(((bf16[16,32,128]{2,1,0:T(8,128)(2,1)}), bf16[16,32,1024]{2,1,0:T(8,128)(2,1)}) %all-gather.10.cloned.1.call-update) | async-done | bytes 1048592 | tf_op jit(solution)/shard_map/all_gather | solution.py:95
  134.7 3.9 multiply_reduce_fusion.3
  138.6 7.5 %psum.106 = f32[512]{0:T(512)S(1)} all-reduce(f32[512]{0:T(512)S(1)} %get-tuple-element.77), channel_id=1, replica_groups=mesh['fsdp'=8,'head'=2,'tensor'=2] {'head','tensor'}, use_global_device_ids=true, to_apply=%region_7.8 | all-reduce | flops 512 | bytes 4096 | tf_op jit(solution)/shard_map/psum | solution.py:144
  146.1 4.3 fusion.45
  150.4 1.3 copy.137
  151.8 2.9 reshape_reshape.8
  154.7 2.4 multiply_reduce_fusion.14
  157.0 3.2 convolution_bitcast_fusion.1
  160.5 1.9 convolution_bitcast_fusion.2
  163.0 11.3 %fusion.9 = (f32[2,256,16]{1,2,0:T(8,128)}, f32[2,256,16]{1,2,0:T(8,128)}, f32[2,256,16]{1,2,0:T(8,128)}, f32[2,256,256]{2,1,0:T(8,128)S(1)}) fusion(f32[2,256,16]{1,2,0:T(8,128)S(1)} %bitcast.243, f32[2,256,16]{1,2,0:T(8,128)S(1)} %copy-done.21, f32[2,256,256]{2,1,0:T(8,128)S(1)} %copy-done.16, pred[256,256]{1,0:T(8,128)(4,1)S(1)} %copy-done.24, ...), kind=kOutput, calls=%fused_computation.18 | convolution fusion | flops 836608000 | bytes 2850816 | tf_op jit(solution)/shard_map/transpose(jvp(clsh,cshp->clhp))/dot_general | solution.py:45
  174.3 0.9 multiply_reduce_fusion.2
  175.2 8.1 %fusion.41 = f32[2,256,16,32]{1,3,2,0:T(8,128)} fusion(f32[2,256,16]{1,2,0:T(8,128)S(1)} %bitcast.244, f32[2,256,16]{1,2,0:T(8,128)S(1)} %copy-done.21, f32[2,256,256]{2,1,0:T(8,128)S(1)} %copy-done.16, pred[256,256]{1,0:T(8,128)(4,1)S(1)} %copy-done.24, f32[2,256,16,32]{1,3,2,0:T(8,128)S(1)} %fusion.58, f32[2,16,32,256]{3,0,2,1:T(2,128)S(1)} %bitcast.208, ...), kind=kOutput, calls=%fused_computation.48 | convolution fusion | flops 816316416 | bytes 3833856 | tf_op jit(solution)/shard_map/transpose(jvp(clsh,cshp->clhp))/dot_general | solution.py:45
  183.3 1.4 convolution_add_fusion.2
  184.7 1.1 convolution_add_fusion.1
  186.8 0.9 add_bitcast_fusion.1
  187.7 5.0 reduce-window.16
  192.9 0.9 fusion.110
  194.5 0.8 reduce_sum.261
  195.4 2.0 copy.140
  197.5 1.1 copy.178
  198.5 2.5 copy.141
  201.1 4.2 multiply_reduce_fusion.7
  207.1 2.0 fusion.117
  209.2 2.1 fusion.118
  211.2 0.8 pad_maximum_fusion
  212.1 8.0 %all-reduce.25 = (bf16[512,16]{0,1:T(8,128)(2,1)S(1)}, f32[16]{0:T(128)S(1)}, f32[16]{0:T(128)S(1)}, f32[16]{0:T(128)S(1)}) all-reduce(f32[512,16]{0,1:T(8,128)S(1)} %get-tuple-element.104, f32[16]{0:T(128)S(1)} %get-tuple-element.103, f32[16]{0:T(128)S(1)} %negate_multiply_fusion, ...), channel_id=1, replica_groups=mesh['fsdp'=8,'head'=2,'tensor'=2] {'tensor'}, use_global_device_ids=true, to_apply=%region_15.16 | all-reduce | flops 8240 | bytes 49536 | tf_op jit(solution)/shard_map/psum | solution.py:154
  220.1 4.0 multiply_add_fusion
  224.2 58.5 %all-reduce.28.cloned.1.call-done = (f32[512,1024]{1,0:T(8,128)}, f32[512,256]{1,0:T(8,128)}) async-done(((f32[512,1024]{1,0:T(8,128)}, f32[512,256]{1,0:T(8,128)}), (f32[512,1024]{1,0:T(8,128)}, f32[512,256]{1,0:T(8,128)})) %all-reduce.28.cloned.1.call-update) | async-done | bytes 2621456 | tf_op jit(solution)/shard_map/psum | solution.py:173
  282.6 2.5 multiply_reduce_fusion.13
  285.5 1.6 fusion.95
  287.5 3.3 fusion.93
  290.9 1.0 fusion.82
  292.0 2.2 fusion.99
  294.2 3.4 fusion.92
  297.7 2.2 fusion.97
  300.1 2.6 fusion.31
  302.8 38.3 %all-reduce.23 = (f32[1024]{0:T(1024)}, f32[16,32,4]{1,0,2:T(8,128)S(1)}, f32[2,128,4]{1,2,0:T(4,128)}, f32[16]{0:T(128)}, f32[16]{0:T(128)}, /*index=5*/f32[16]{0:T(128)}, f32[16,32]{1,0:T(8,128)}) all-reduce(f32[1024]{0:T(1024)S(1)} %get-tuple-element.74, ...), channel_id=1, replica_groups=mesh['fsdp'=8,'head'=2,'tensor'=2] {'fsdp'}, use_global_device_ids=true, to_apply=%region_21.22 | all-reduce | flops 4656 | bytes 37248 | tf_op jit(solution)/shard_map/psum | solution.py:206
  341.6 10.1 %reduce-scatter.10.cloned.1.call-done = f32[128,256]{1,0:T(8,128)} async-done(((f32[1024,256]{1,0:T(8,128)}), f32[128,256]{1,0:T(8,128)}) %reduce-scatter.10.cloned.1.call-update) | async-done | bytes 131088 | tf_op jit(solution)/shard_map/reduce_scatter | solution.py:196
  351.7 1.6 reshape.276
  353.3 57.6 %all-gather.12.cloned.1.call-done = f32[2048,1024]{1,0:T(8,128)} async-done(((f32[512,1024]{1,0:T(8,128)}), f32[2048,1024]{1,0:T(8,128)}) %all-gather.12.cloned.1.call-update) | async-done | bytes 8388624 | tf_op jit(solution)/shard_map/all_gather | solution.py:125
  410.9 5.9 reduce_sum.225
  416.8 4.3 fusion.28
  421.1 48.3 %reduce-scatter.12.cloned.1.call-done = f32[128,16]{0,1:T(8,128)} async-done(((f32[1024,16]{0,1:T(8,128)}), f32[128,16]{0,1:T(8,128)}) %reduce-scatter.12.cloned.1.call-update) | async-done | bytes 8208 | tf_op jit(solution)/shard_map/reduce_scatter | solution.py:197
  469.4 72.1 %reduce-scatter.6.cloned.1.call-done = f32[128,16,32]{0,2,1:T(8,128)} async-done(((f32[1024,16,32]{0,2,1:T(8,128)}), f32[128,16,32]{0,2,1:T(8,128)}) %reduce-scatter.6.cloned.1.call-update) | async-done | bytes 262160 | tf_op jit(solution)/shard_map/reduce_scatter | solution.py:184
  541.5 72.0 %reduce-scatter.14.cloned.1.call-done = f32[16,32,128]{2,1,0:T(8,128)} async-done(((f32[16,32,1024]{2,1,0:T(8,128)}), f32[16,32,128]{2,1,0:T(8,128)}) %reduce-scatter.14.cloned.1.call-update) | async-done | bytes 262160 | tf_op jit(solution)/shard_map/reduce_scatter | solution.py:198
  613.5 72.1 %reduce-scatter.8.cloned.1.call-done = f32[128,16,32]{0,2,1:T(8,128)} async-done(((f32[1024,16,32]{0,2,1:T(8,128)}), f32[128,16,32]{0,2,1:T(8,128)}) %reduce-scatter.8.cloned.1.call-update) | async-done | bytes 262160 | tf_op jit(solution)/shard_map/reduce_scatter | solution.py:190
  (187 shorter events, 14.9 us)
Async XLA Ops:
  7.2 39.7 %copy-start.30 = (f32[16,32,4]{1,2,0:T(4,128)S(1)}, f32[16,32,4]{1,2,0:T(4,128)}, u32[]{:S(2)}) copy-start(f32[16,32,4]{1,2,0:T(4,128)} %param.21) | copy-start | bytes 24580
  7.2 39.8 %copy-start.22 = (bf16[128,2,128]{2,1,0:T(2,128)(2,1)S(1)}, bf16[128,2,128]{2,1,0:T(2,128)(2,1)}, u32[]{:S(2)}) copy-start(bf16[128,2,128]{2,1,0:T(2,128)(2,1)} %param.19) | copy-start | bytes 196612
  7.2 75.7 %all-gather.6.cloned.1.call-start = ((), (), s32[]{:S(2)}) async-start(), calls=%async_computation.5 | async-start | bytes 1179648 | tf_op jit(solution)/shard_map/all_gather | solution.py:91
  7.9 90.7 %all-gather.8.cloned.1.call-start = ((), (), s32[]{:S(2)}) async-start(), calls=%async_computation.6 | async-start | bytes 1179648 | tf_op jit(solution)/shard_map/all_gather | solution.py:92
  8.7 126.0 %all-gather.10.cloned.1.call-start = ((), (), s32[]{:S(2)}) async-start(), calls=%async_computation.7 | async-start | bytes 1179648 | tf_op jit(solution)/shard_map/all_gather | solution.py:95
  9.4 70.0 %copy-start = (bf16[512,1024]{1,0:T(8,128)(2,1)S(1)}, bf16[512,1024]{1,0:T(8,128)(2,1)}, u32[]{:S(2)}) copy-start(bf16[512,1024]{1,0:T(8,128)(2,1)} %param.14) | copy-start | bytes 3145732
  9.4 70.0 %copy-start.25 = (f32[1024]{0:T(1024)S(1)}, f32[1024]{0:T(1024)}, u32[]{:S(2)}) copy-start(f32[1024]{0:T(1024)} %param.16) | copy-start | bytes 12292
  9.4 273.2 %all-reduce.28.cloned.1.call-start = ((), (), s32[]{:S(2)}) async-start(), calls=%async_computation.14 | async-start | bytes 5242880 | tf_op jit(solution)/shard_map/psum | solution.py:173
  39.7 3.0 copy-start.18
  40.4 3.7 copy-start.56
  44.1 35.9 %copy-start.54 = (f32[2,128,4]{1,2,0:T(4,128)S(1)}, f32[2,128,4]{1,2,0:T(4,128)}, u32[]{:S(2)}) copy-start(f32[2,128,4]{1,2,0:T(4,128)} %param.22) | copy-start | bytes 12292
  44.2 45.8 %copy-start.20 = (f32[2,256,16]{1,2,0:T(8,128)}, f32[2,256,16]{1,2,0:T(8,128)S(1)}, u32[]{:S(2)}) copy-start(f32[2,256,16]{1,2,0:T(8,128)S(1)} %bitcast_bitcast_fusion.1) | copy-start | bytes 98308
  47.0 38.1 %copy-start.34 = (f32[512,1]{0,1:T(1,128)}, f32[512,1]{0,1:T(1,128)S(1)}, u32[]{:S(2)}) copy-start(f32[512,1]{0,1:T(1,128)S(1)} %get-tuple-element.131) | copy-start | bytes 6148
  47.0 38.1 %copy-start.36 = (f32[512,1]{0,1:T(1,128)}, f32[512,1]{0,1:T(1,128)S(1)}, u32[]{:S(2)}) copy-start(f32[512,1]{0,1:T(1,128)S(1)} %get-tuple-element.132) | copy-start | bytes 6148
  47.0 38.1 %copy-start.38 = (f32[512,1]{0,1:T(1,128)}, f32[512,1]{0,1:T(1,128)S(1)}, u32[]{:S(2)}) copy-start(f32[512,1]{0,1:T(1,128)S(1)} %get-tuple-element.133) | copy-start | bytes 6148
  47.0 38.1 %copy-start.40 = (f32[512,1]{0,1:T(1,128)}, f32[512,1]{0,1:T(1,128)S(1)}, u32[]{:S(2)}) copy-start(f32[512,1]{0,1:T(1,128)S(1)} %get-tuple-element.134) | copy-start | bytes 6148
  79.5 1.7 copy-start.57
  79.5 2.5 copy-start.53
  80.0 5.0 copy-start.44
  80.0 5.0 copy-start.46
  80.0 5.0 copy-start.48
  80.0 5.0 copy-start.50
  82.8 7.2 %copy-start.15 = (f32[2,256,256]{2,1,0:T(8,128)}, f32[2,256,256]{2,1,0:T(8,128)S(1)}, u32[]{:S(2)}) copy-start(f32[2,256,256]{2,1,0:T(8,128)S(1)} %fusion.116) | copy-start | bytes 1572868
  87.6 11.0 %copy-start.2 = (bf16[512,512]{1,0:T(8,128)(2,1)}, bf16[512,512]{1,0:T(8,128)(2,1)S(1)}, u32[]{:S(2)}) copy-start(bf16[512,512]{1,0:T(8,128)(2,1)S(1)} %get-tuple-element.107) | copy-start | bytes 1572868
  88.0 8.4 %copy-start.8 = (bf16[2,256,16,32]{1,0,3,2:T(2,128)(2,1)}, bf16[2,256,16,32]{1,0,3,2:T(2,128)(2,1)S(1)}, u32[]{:S(2)}) copy-start(bf16[2,256,16,32]{1,0,3,2:T(2,128)(2,1)S(1)} %reshape_reshape.7) | copy-start | bytes 1572868
  88.0 2.0 copy-start.23
  88.0 2.0 copy-start.31
  89.9 6.4 copy-start.5
  97.2 1.4 copy-start.42
  98.6 36.1 %copy-start.26 = (f32[512]{0:T(512)S(1)}, f32[512]{0:T(512)}, u32[]{:S(2)}) copy-start(f32[512]{0:T(512)} %mul.547) | copy-start | bytes 6148
  110.2 35.9 %copy-start.28 = (f32[512]{0:T(512)}, f32[512]{0:T(512)S(1)}, u32[]{:S(2)}) copy-start(f32[512]{0:T(512)S(1)} %get-tuple-element.142) | copy-start | bytes 6148
  154.6 5.6 copy-start.1
  154.6 5.6 copy-start.6
  157.0 3.5 copy-start.9
  157.0 3.5 copy-start.33
  160.5 2.5 copy-start.16
  160.5 2.5 copy-start.21
  160.5 2.5 copy-start.24
  160.5 2.5 copy-start.32
  197.4 3.6 copy-start.43
  201.1 4.3 copy-start.35
  201.1 4.3 copy-start.37
  201.1 4.3 copy-start.39
  201.1 4.3 copy-start.41
  205.9 1.2 copy-start.11
  207.1 2.0 copy-start.3
  207.1 2.0 copy-start.12
  209.2 2.1 copy-start.13
  209.2 2.1 copy-start.14
  209.2 10.9 %copy-start.19 = (bf16[1024,16]{0,1:T(8,128)(2,1)S(1)}, bf16[1024,16]{0,1:T(8,128)(2,1)}, u32[]{:S(2)}) copy-start(bf16[1024,16]{0,1:T(8,128)(2,1)} %copy-done.18) | copy-start | bytes 98308
  224.1 61.0 %copy-start.45 = (f32[256,1]{0,1:T(1,128)S(1)}, f32[256,1]{0,1:T(1,128)}, u32[]{:S(2)}) copy-start(f32[256,1]{0,1:T(1,128)} %copy-done.44) | copy-start | bytes 3076
  224.1 61.0 %copy-start.47 = (f32[256,1]{0,1:T(1,128)S(1)}, f32[256,1]{0,1:T(1,128)}, u32[]{:S(2)}) copy-start(f32[256,1]{0,1:T(1,128)} %copy-done.46) | copy-start | bytes 3076
  224.1 61.1 %copy-start.49 = (f32[256,1]{0,1:T(1,128)S(1)}, f32[256,1]{0,1:T(1,128)}, u32[]{:S(2)}) copy-start(f32[256,1]{0,1:T(1,128)} %copy-done.48) | copy-start | bytes 3076
  224.1 61.1 %copy-start.51 = (f32[256,1]{0,1:T(1,128)S(1)}, f32[256,1]{0,1:T(1,128)}, u32[]{:S(2)}) copy-start(f32[256,1]{0,1:T(1,128)} %copy-done.50) | copy-start | bytes 3076
  224.1 127.6 %reduce-scatter.10.cloned.1.call-start = ((), (), s32[]{:S(2)}) async-start(), calls=%async_computation.10 | async-start | bytes 1179648 | tf_op jit(solution)/shard_map/reduce_scatter | solution.py:196
  285.5 1.9 copy-start.27
  285.5 1.9 copy-start.29
  287.1 123.8 %all-gather.12.cloned.1.call-start = ((), (), s32[]{:S(2)}) async-start(), calls=%async_computation.13 | async-start | bytes 10485760 | tf_op jit(solution)/shard_map/all_gather | solution.py:125
  290.8 178.6 %reduce-scatter.12.cloned.1.call-start = ((), (), s32[]{:S(2)}) async-start(), calls=%async_computation.11 | async-start | bytes 73728 | tf_op jit(solution)/shard_map/reduce_scatter | solution.py:197
  291.9 249.6 %reduce-scatter.6.cloned.1.call-start = ((), (), s32[]{:S(2)}) async-start(), calls=%async_computation.8 | async-start | bytes 2359296 | tf_op jit(solution)/shard_map/reduce_scatter | solution.py:184
  294.1 319.3 %reduce-scatter.14.cloned.1.call-start = ((), (), s32[]{:S(2)}) async-start(), calls=%async_computation.12 | async-start | bytes 2359296 | tf_op jit(solution)/shard_map/reduce_scatter | solution.py:198
  297.6 2.4 copy-start.55
  297.6 388.0 %reduce-scatter.8.cloned.1.call-start = ((), (), s32[]{:S(2)}) async-start(), calls=%async_computation.9 | async-start | bytes 2359296 | tf_op jit(solution)/shard_map/reduce_scatter | solution.py:190
  410.9 5.9 copy-start.52
  (4 other events, 3.7 us)
Sparse Core Ops, SparseCore 0:
  10.0 43.5 all-gather.5
  55.7 38.4 all-gather.7
  96.3 38.3 all-gather.9
  224.2 58.3 all-reduce.27
  287.3 64.4 reduce-scatter.9
  353.7 57.1 all-gather.11
  414.6 54.7 reduce-scatter.11
  473.5 67.9 reduce-scatter.5
  545.6 67.8 reduce-scatter.13
  617.4 68.1 reduce-scatter.7
